TPU v7x, 128 devices: a whole 4x4x4 slice. The times are simulated.
128 devices in a mesh: kt: 8 (over x_hi, z), ks: 16 (over y, x_lo, core).
Axes of the slice: x: 4 (x_hi: 2, x_lo: 2; x = x_hi * 2 + x_lo), y: 4, z: 4, core: 2. Of those that a mesh axis runs over, the one named last changes fastest.
Arguments:
- val_target: bfloat16 [16, 32, 512], P('kt', None, 'ks'), may hold values from -6 to 6
- cond_target: bfloat16 [16, 64, 512], P('kt', None, 'ks'), may hold values from -0.03125 to 0.03125
- val_source: bfloat16 [64, 32, 512], P('ks', None, 'kt'), may hold values from -6 to 6
- cond_source: bfloat16 [64, 64, 512], P('ks', None, 'kt'), may hold values from -0.125 to 0.125
- trial_vectors: bfloat16 [64, 16, 2048], P('ks', 'kt'), may hold values from -6 to 6
- screened: bfloat16 [512, 512, 512], P(None, ('kt', 'ks')), may hold values from -0.25 to 0.25
- pair_momentum: int32 [16, 64], replicated, may hold values from 0 to 511
Outputs:
- kernel_out: float32 [16, 16, 2048], P('kt', 'ks')
All inputs are finite; a program needn't handle non-finite values.
Results may differ from a plain program's by a relative error of at most 0.019.
Values may be sent and summed in bfloat16 or wider, within the bound.
No kernel may reach another device: no remote copies, remote signals or barrier semaphores. Data moves between devices by JAX's collectives and lax.ppermute only.
A program may use at most 128 MiB of HBM per device.

v0:
```python
import jax
import jax.numpy as jnp
from jax import lax
from jax.sharding import PartitionSpec as P


def rows_first(arrays, axis, dims):
    turned = [jnp.moveaxis(a, dim, 0) for a, dim in zip(arrays, dims)]
    both = jnp.concatenate([t.reshape(len(t), -1) for t in turned], axis=1)
    whole, at, finished = (lax.all_gather(both, axis, axis=0, tiled=True), 0, [])
    for t, dim in zip(turned, dims):
        slab = whole[:, at : at + t[0].size].reshape(-1, *t.shape[1:])
        finished.append(jnp.moveaxis(slab, 0, dim))
        at += t[0].size
    return tuple(finished)


def sent_together(arrays, axis, dim, along):
    ends, at = ([], 0)
    for a in arrays[:-1]:
        at += a.shape[along]
        ends.append(at)
    both = jnp.concatenate(arrays, axis=along)
    return tuple(jnp.split(lax.all_gather(both, axis, axis=dim, tiled=True), ends, axis=along))


def cut_along(x, dim, peers):
    before, after = (x.shape[:dim], x.shape[dim + 1 :])
    return jnp.moveaxis(x.reshape(*before, peers, -1, *after), dim, 0)


def sum_at_owner(x, axis, dim):
    blocks = cut_along(x, dim, lax.axis_size(axis))
    arrived = lax.all_to_all(blocks, axis, split_axis=0, concat_axis=0, tiled=True)
    return arrived.astype(jnp.float32).sum(axis=0)


def local(val_target, cond_target, val_source, cond_source, trial_vectors, screened, pair_momentum):
    tgt_val, tgt_cond = rows_first((val_target, cond_target), "ks", (2, 2))
    src_val, src_cond, vectors = (
        *sent_together((val_source, cond_source), "kt", 2, 1),
        lax.all_gather(trial_vectors, "kt", axis=1, tiled=True),
    )
    count_kt = lax.axis_size("kt")
    count_ks = lax.axis_size("ks")
    tgt_count = tgt_val.shape[0]
    src_count = src_val.shape[0]
    pair_count = tgt_count * src_count
    width = screened.shape[2]
    val_bands = tgt_val.shape[1]
    cond_bands = tgt_cond.shape[1]
    vec_count = vectors.shape[1]
    table = pair_momentum.reshape(count_kt, tgt_count, count_ks, src_count)
    table = table.transpose(1, 3, 0, 2).reshape(pair_count, count_kt * count_ks)
    outgoing = screened[table]
    arrived = lax.all_to_all(outgoing, ("kt", "ks"), split_axis=1, concat_axis=1, tiled=True)
    pair_mats = arrived.reshape(tgt_count, src_count, width, width)
    trial_four = vectors.reshape(src_count, vec_count, val_bands, cond_bands)
    dressed = jnp.einsum(
        "snwc,scq->snwq", trial_four, src_cond, preferred_element_type=jnp.float32
    ).astype(jnp.bfloat16)
    pair_prod = (
        tgt_val.astype(jnp.float32)[:, None, :, None, :]
        * src_val.astype(jnp.float32)[None, :, None, :, :]
    ).astype(jnp.bfloat16)
    kernels = jnp.einsum(
        "tsvwp,tspq->tsvwq", pair_prod, pair_mats, preferred_element_type=jnp.float32
    ).astype(jnp.bfloat16)
    reduced = jnp.einsum(
        "tsvwq,snwq->tvnq", kernels, dressed, preferred_element_type=jnp.float32
    ).astype(jnp.bfloat16)
    partial_out = jnp.einsum(
        "tvnq,tcq->tnvc", reduced, tgt_cond, preferred_element_type=jnp.float32
    )
    partial_out = partial_out.reshape(tgt_count, vec_count, val_bands * cond_bands)
    return sum_at_owner(partial_out.astype(jnp.bfloat16), "ks", 1)


def solution(mesh):
    in_specs = (
        P("kt", None, "ks"),
        P("kt", None, "ks"),
        P("ks", None, "kt"),
        P("ks", None, "kt"),
        P("ks", "kt", None),
        P(None, ("kt", "ks"), None),
        P(),
    )
    out_specs = P("kt", "ks", None)
    return jax.shard_map(local, mesh=mesh, in_specs=in_specs, out_specs=out_specs, check_vma=False)
```

profile of v0, /device:TPU:1, one launch (start us, length us, event | category | flops | bytes accessed | tf_op | source)
XLA Modules:
  0.0 284.5 jit_solution(2779591411790372973)
XLA Ops:
  0.0 0.0 copy-start
  0.0 0.9 reshape.72
  1.0 0.2 copy.98
  1.1 0.1 reshape.73
  1.2 0.4 copy-done
  1.6 10.8 %gather_fusion = bf16[1024,4,512]{2,1,0:T(4,128)(2,1)} fusion(bf16[512,4,512]{2,1,0:T(4,128)(2,1)S(1)} %copy-done, s32[1024]{0:T(1024)S(1)} %fusion.16), kind=kCustom, calls=%fused_computation | custom fusion | bytes 8392704 | tf_op jit(solution)/shard_map/gather | solution.py:55
  12.4 6.5 %copy.100 = bf16[8,128,4,512]{3,2,0,1:T(4,128)(2,1)} copy(bf16[8,128,4,512]{3,2,1,0:T(4,128)(2,1)} %bitcast.54) | data formatting | bytes 8388608 | tf_op jit(solution)/shard_map/gather | solution.py:55
  18.9 0.0 copy-start.6
  18.9 0.0 copy-start.5
  18.9 12.0 %all-to-all-start = ((bf16[8,128,4,512]{3,2,0,1:T(4,128)(2,1)}), bf16[8,128,4,512]{3,2,0,1:T(4,128)(2,1)}, u32[]{:S(2)}, u32[]{:S(2)}) async-start(bf16[8,128,4,512]{3,2,0,1:T(4,128)(2,1)} %copy.100), calls=%async_computation | async-start | bytes 8388608 | tf_op jit(solution)/shard_map/all_to_all | solution.py:56
  30.9 0.0 copy-start.4
  30.9 0.0 copy-done.6
  30.9 0.1 reshape.69
  31.0 0.0 copy-done.5
  31.0 0.1 copy.111
  31.1 0.1 pad_maximum_fusion.1
  31.2 59.9 %all_gather.9 = bf16[512,192]{1,0:T(8,128)(2,1)S(1)} all-gather(bf16[32,192]{1,0:T(8,128)(2,1)S(1)} %pad_maximum_fusion.1), channel_id=1, replica_groups=mesh['kt'=8,'ks'=16] {'ks'}, dimensions={0}, use_global_device_ids=true | all-gather | bytes 208896 | tf_op jit(solution)/shard_map/all_gather | solution.py:10
  91.1 0.1 slice.10
  91.3 0.0 copy-done.3
  91.3 0.1 copy.91
  91.4 0.0 copy-done.2
  91.4 0.1 copy.92
  91.5 0.1 pad_maximum_fusion
  91.6 30.6 %all_gather.10 = bf16[4,96,512]{1,0,2:T(4,128)(2,1)S(1)} all-gather(bf16[4,96,64]{1,0,2:T(4,128)(2,1)S(1)} %pad_maximum_fusion), channel_id=1, replica_groups=mesh['kt'=8,'ks'=16] {'kt'}, dimensions={2}, use_global_device_ids=true | all-gather | bytes 442368 | tf_op jit(solution)/shard_map/all_gather | solution.py:24
  122.2 0.4 split.8
  122.6 0.3 copy.118
  122.9 0.1 copy.117
  123.0 0.3 copy.116
  123.3 0.0 copy-done.4
  123.3 28.7 %all_gather.11 = bf16[4,16,2048]{2,0,1:T(4,128)(2,1)S(1)} all-gather(bf16[4,2,2048]{2,0,1:T(4,128)(2,1)S(1)} %copy.94), channel_id=1, replica_groups=mesh['kt'=8,'ks'=16] {'kt'}, dimensions={1}, use_global_device_ids=true | all-gather | bytes 294912 | tf_op jit(solution)/shard_map/all_gather | solution.py:42
  152.1 0.1 copy.95
  152.2 0.5 reshape.71
  152.7 0.7 convert_bitcast_fusion
  153.4 12.2 %copy.108 = bf16[4,16,32,512,1]{2,1,0,4,3:T(8,128)(2,1)} copy(bf16[4,16,32,512,1]{3,2,1,0,4:T(8,128)(2,1)S(1)} %convert_bitcast_fusion) | data formatting | bytes 4194304 | tf_op jit(solution)/shard_map/convert_element_type | solution.py:61
  165.6 0.1 copy.90
  165.7 0.0 all-to-all-done
  165.7 5.6 %copy.101 = bf16[8,128,4,512]{3,2,1,0:T(4,128)(2,1)} copy(bf16[8,128,4,512]{3,2,0,1:T(4,128)(2,1)} %all-to-all-done) | data formatting | bytes 8388608 | tf_op jit(solution)/shard_map/all_to_all | solution.py:56
  171.3 6.9 %reshape.86 = bf16[2,4,512,512,1]{3,2,1,0,4:T(8,128)(2,1)} reshape(bf16[8,128,4,512]{3,2,1,0:T(4,128)(2,1)} %copy.101) | data formatting | bytes 8388608 | tf_op jit(solution)/shard_map/reshape | solution.py:57
  178.2 8.9 %fusion.3 = bf16[2,4,32,32,512]{4,3,2,1,0:T(8,128)(2,1)} fusion(f32[4,32,512]{2,1,0:T(8,128)S(1)} %convert_element_type.54, f32[2,32,512]{2,1,0:T(8,128)S(1)} %convert_bitcast_fusion.1, bf16[2,4,512,512,1]{3,2,1,0,4:T(8,128)(2,1)} %reshape.86), kind=kOutput, calls=%fused_computation.6 | convolution fusion | flops 4307550208 | bytes 12976128 | tf_op jit(solution)/shard_map/tsvwp,tspq->tsvwq/dot_general | solution.py:66
  187.1 44.3 %copy.103 = bf16[2,4,32,32,512]{3,2,1,0,4:T(8,128)(2,1)} copy(bf16[2,4,32,32,512]{4,3,2,1,0:T(8,128)(2,1)} %fusion.3) | data formatting | bytes 16777216 | tf_op jit(solution)/shard_map/convert_element_type | solution.py:68
  231.4 28.3 %fusion.4 = bf16[2,32,16,512]{1,2,0,3:T(8,128)(2,1)} fusion(bf16[4,16,32,512,1]{2,1,0,4,3:T(8,128)(2,1)} %copy.108, bf16[2,4,32,32,512]{3,2,1,0,4:T(8,128)(2,1)} %copy.103), kind=kOutput, calls=%fused_computation.7 | convolution fusion | flops 134742016 | bytes 11534336 | tf_op jit(solution)/shard_map/tsvwq,snwq->tvnq/dot_general | solution.py:69
  259.8 3.7 %fusion.11 = bf16[2,16,32,64]{3,2,1,0:T(8,128)(2,1)S(1)} fusion(bf16[2,64,512,1]{2,1,3,0:T(8,128)(2,1)S(1)} %bitcast.56, bf16[2,32,16,512]{1,2,0,3:T(8,128)(2,1)} %fusion.4), kind=kOutput, calls=%fused_computation.13 | convolution fusion | flops 67174400 | bytes 1310720 | tf_op jit(solution)/shard_map/tvnq,tcq->tnvc/dot_general | solution.py:72
  263.5 0.3 convert_element_type.61
  263.7 0.1 copy.126
  263.9 19.9 %all_to_all.10 = bf16[16,2,1,2048]{3,1,2,0:T(2,128)(2,1)S(1)} all-to-all(bf16[16,2,1,2048]{3,1,2,0:T(2,128)(2,1)S(1)} %bitcast.58), channel_id=1, replica_groups=mesh['kt'=8,'ks'=16] {'ks'}, dimensions={0} | all-to-all | bytes 262144 | tf_op jit(solution)/shard_map/all_to_all | solution.py:34
  283.8 0.1 convert_reduce_fusion
  283.9 0.6 reduce_sum.12
  284.5 0.0 copy-done.1
  (9 shorter events, 0.1 us)
Async XLA Ops:
  0.0 1.6 copy-start
  18.9 12.0 %copy-start.6 = (bf16[2,64,32]{1,2,0:T(8,128)(2,1)S(1)}, bf16[2,64,32]{1,2,0:T(8,128)(2,1)}, u32[]{:S(2)}) copy-start(bf16[2,64,32]{1,2,0:T(8,128)(2,1)} %param.8) | copy-start | bytes 24580
  18.9 12.1 %copy-start.5 = (bf16[2,32,32]{2,1,0:T(8,128)(2,1)S(1)}, bf16[2,32,32]{2,1,0:T(8,128)(2,1)}, u32[]{:S(2)}) copy-start(bf16[2,32,32]{2,1,0:T(8,128)(2,1)} %param.7) | copy-start | bytes 12292
  18.9 72.3 %copy-start.3 = (bf16[4,32,64]{2,1,0:T(8,128)(2,1)S(1)}, bf16[4,32,64]{2,1,0:T(8,128)(2,1)}, u32[]{:S(2)}) copy-start(bf16[4,32,64]{2,1,0:T(8,128)(2,1)} %param.9) | copy-start | bytes 49156
  18.9 72.5 %copy-start.2 = (bf16[4,64,64]{2,1,0:T(8,128)(2,1)S(1)}, bf16[4,64,64]{2,1,0:T(8,128)(2,1)}, u32[]{:S(2)}) copy-start(bf16[4,64,64]{2,1,0:T(8,128)(2,1)} %param.10) | copy-start | bytes 98308
  18.9 146.8 %all-to-all-start = ((bf16[8,128,4,512]{3,2,0,1:T(4,128)(2,1)}), bf16[8,128,4,512]{3,2,0,1:T(4,128)(2,1)}, u32[]{:S(2)}, u32[]{:S(2)}) async-start(bf16[8,128,4,512]{3,2,0,1:T(4,128)(2,1)} %copy.100), calls=%async_computation | async-start | bytes 8388608 | tf_op jit(solution)/shard_map/all_to_all | solution.py:56
  30.9 92.4 %copy-start.4 = (bf16[4,2,2048]{2,1,0:T(2,128)(2,1)S(1)}, bf16[4,2,2048]{2,1,0:T(2,128)(2,1)}, u32[]{:S(2)}) copy-start(bf16[4,2,2048]{2,1,0:T(2,128)(2,1)} %param.11) | copy-start | bytes 98308
  231.4 53.1 %copy-start.1 = (bf16[512,4,512]{2,1,0:T(4,128)(2,1)S(1)}, bf16[512,4,512]{2,1,0:T(4,128)(2,1)}, u32[]{:S(2)}) copy-start(bf16[512,4,512]{2,1,0:T(4,128)(2,1)} %param.12) | copy-start | bytes 6291460
where the time goes:
time: 285 us; the launch traced here: 284 us
  blocking collectives  139 us (49%)
  local copies, waits for them, and re-layouts  91.2 us (32%)
  matrix products  41.6 us (15%)
  starting transfers between devices  12 us (4%)
    all_gather x1, blocking collectives, rows_first(): lax.all_gather(both, axis, axis=0, tiled=True)  59.9 us
    convert_element_type x1, local copies, waits for them, and re-layouts, local(): kernels = jnp.einsum('tsvwp,tspq->tsvwq', pair_prod, pair_mats, preferred...  44.3 us
    all_gather x1, blocking collectives, sent_together(): lax.all_gather(both, axis, axis=dim, tiled=True)  30.6 us
    all_gather x1, blocking collectives, local(): lax.all_gather(trial_vectors, 'kt', axis=1, tiled=True)  28.7 us
    dot_general x1, matrix products, local(): jnp.einsum('tsvwq,snwq->tvnq', kernels, dressed, preferred_element_type=j...  28.3 us
    all_to_all x1, blocking collectives, sum_at_owner(): lax.all_to_all(blocks, axis, split_axis=0, concat_axis=0, tiled=True)  19.9 us
    gather x2, local copies, waits for them, and re-layouts, local(): outgoing = screened[table]  17.3 us
    convert_element_type x1, local copies, waits for them, and re-layouts, local(): dressed = jnp.einsum('snwc,scq->snwq', trial_four, src_cond, preferred_el...  12.2 us
  transfers between devices with their start and end apart: 1, of which 0 were waited for; matrix products, arithmetic and copies ran while one was open for 5% of the time, Pallas kernels for 0%

commit v1 on v0

--- a/solution.py
+++ b/solution.py
@@ -1,7 +1,19 @@
+import functools
 import jax
 import jax.numpy as jnp
 from jax import lax
 from jax.sharding import PartitionSpec as P
+
+
+def solve_the_surface(frame_in, join_dim):
+    parts_seen = []
+    for _ in range(lax.axis_size("kt")):
+        parts_seen.append(frame_in)
+    z2 = lax.all_to_all(jnp.stack(parts_seen, axis=0), axis_name="kt", split_axis=0, concat_axis=0)
+    return jnp.concatenate(z2, axis=join_dim)
+
+
+name_the_words = functools.partial(solve_the_surface, join_dim=1)
 
 
 def rows_first(arrays, axis, dims):
@@ -39,7 +51,7 @@
     tgt_val, tgt_cond = rows_first((val_target, cond_target), "ks", (2, 2))
     src_val, src_cond, vectors = (
         *sent_together((val_source, cond_source), "kt", 2, 1),
-        lax.all_gather(trial_vectors, "kt", axis=1, tiled=True),
+        name_the_words(trial_vectors),
     )
     count_kt = lax.axis_size("kt")
     count_ks = lax.axis_size("ks")

time: 285 us -> 259 us (0.909)
  blocking collectives: 139 us -> 105 us
  starting transfers between devices: 12 us -> 19.2 us
    all_gather x1 -> x0, blocking collectives: 28.7 us -> none  [local(): lax.all_gather(trial_vectors, 'kt', axis=1, tiled=True)]
    all_to_all x0 -> x1, starting transfers between devices: none -> 8.32 us  [solve_the_surface(): lax.all_to_all(jnp.stack(parts_seen, axis=0), axis_name='kt', split_axis=...]
    all_to_all x1, blocking collectives: 19.9 us -> 14.2 us  [sum_at_owner(): lax.all_to_all(blocks, axis, split_axis=0, concat_axis=0, tiled=True)]
  transfers between devices with their start and end apart: 1 -> 2, of which waited for: 0 -> 0; matrix products, arithmetic and copies ran while one was open for 5% -> 13% of each run, Pallas kernels for 0% -> 0%
where the time goes in v1:
time: 259 us; the launch traced here: 258 us
  blocking collectives  105 us (41%)
  local copies, waits for them, and re-layouts  92.4 us (36%)
  matrix products  41.6 us (16%)
  starting transfers between devices  19.2 us (7%)
    all_gather x1, blocking collectives, rows_first(): lax.all_gather(both, axis, axis=0, tiled=True)  60 us
    convert_element_type x1, local copies, waits for them, and re-layouts, local(): kernels = jnp.einsum('tsvwp,tspq->tsvwq', pair_prod, pair_mats, preferred...  44.3 us
    all_gather x1, blocking collectives, sent_together(): lax.all_gather(both, axis, axis=dim, tiled=True)  30.6 us
    dot_general x1, matrix products, local(): jnp.einsum('tsvwq,snwq->tvnq', kernels, dressed, preferred_element_type=j...  28.3 us
    gather x2, local copies, waits for them, and re-layouts, local(): outgoing = screened[table]  17.3 us
    all_to_all x1, blocking collectives, sum_at_owner(): lax.all_to_all(blocks, axis, split_axis=0, concat_axis=0, tiled=True)  14.2 us
    convert_element_type x1, local copies, waits for them, and re-layouts, local(): dressed = jnp.einsum('snwc,scq->snwq', trial_four, src_cond, preferred_el...  12.2 us
    all_to_all x1, starting transfers between devices, local(): lax.all_to_all(outgoing, ('kt', 'ks'), split_axis=1, concat_axis=1, tiled...  10.8 us
  transfers between devices with their start and end apart: 2, of which 0 were waited for; matrix products, arithmetic and copies ran while one was open for 13% of the time, Pallas kernels for 0%

profile of v1, /device:TPU:1, one launch (start us, length us, event | category | flops | bytes accessed | tf_op | source)
XLA Modules:
  0.0 258.5 jit_solution(3997585238691831217)
XLA Ops:
  0.0 0.0 copy-start
  0.0 1.8 stack.2
  1.8 8.3 %all-to-all-start = ((bf16[8,4,2,2048]{3,2,1,0:T(2,128)(2,1)}), bf16[8,4,2,2048]{3,2,1,0:T(2,128)(2,1)S(1)}, u32[]{:S(2)}, u32[]{:S(2)}) async-start(bf16[8,4,2,2048]{3,2,1,0:T(2,128)(2,1)} %stack.2), calls=%async_computation | async-start | bytes 524288 | tf_op jit(solution)/shard_map/all_to_all | solution.py:12
  10.1 0.8 reshape.74
  10.9 0.2 copy.93
  11.1 0.1 reshape.75
  11.2 0.0 copy-done
  11.2 10.8 %gather_fusion = bf16[1024,4,512]{2,1,0:T(4,128)(2,1)} fusion(bf16[512,4,512]{2,1,0:T(4,128)(2,1)S(1)} %copy-done, s32[1024]{0:T(1024)S(1)} %fusion.16), kind=kCustom, calls=%fused_computation | custom fusion | bytes 8392704 | tf_op jit(solution)/shard_map/gather | solution.py:67
  22.0 6.5 %copy.95 = bf16[8,128,4,512]{3,2,0,1:T(4,128)(2,1)} copy(bf16[8,128,4,512]{3,2,1,0:T(4,128)(2,1)} %bitcast.55) | data formatting | bytes 8388608 | tf_op jit(solution)/shard_map/gather | solution.py:67
  28.5 0.0 copy-start.5
  28.5 0.0 copy-start.4
  28.5 0.0 all-to-all-done
  28.5 10.8 %all-to-all-start.1 = ((bf16[8,128,4,512]{3,2,0,1:T(4,128)(2,1)}), bf16[8,128,4,512]{3,2,0,1:T(4,128)(2,1)}, u32[]{:S(2)}, u32[]{:S(2)}) async-start(bf16[8,128,4,512]{3,2,0,1:T(4,128)(2,1)} %copy.95), calls=%async_computation.1 | async-start | bytes 8388608 | tf_op jit(solution)/shard_map/all_to_all | solution.py:68
  39.4 0.0 copy-done.5
  39.4 0.1 reshape.71
  39.5 0.0 copy-done.4
  39.5 0.1 copy.106
  39.6 0.1 pad_maximum_fusion.1
  39.7 60.0 %all_gather.6 = bf16[512,192]{1,0:T(8,128)(2,1)S(1)} all-gather(bf16[32,192]{1,0:T(8,128)(2,1)S(1)} %pad_maximum_fusion.1), channel_id=1, replica_groups=mesh['kt'=8,'ks'=16] {'ks'}, dimensions={0}, use_global_device_ids=true | all-gather | bytes 208896 | tf_op jit(solution)/shard_map/all_gather | solution.py:22
  99.6 0.1 slice.10
  99.7 0.0 copy-done.3
  99.8 0.1 copy.87
  99.9 0.0 copy-done.2
  99.9 0.1 copy.88
  100.0 0.1 pad_maximum_fusion
  100.1 30.6 %all_gather.7 = bf16[4,96,512]{1,0,2:T(4,128)(2,1)S(1)} all-gather(bf16[4,96,64]{1,0,2:T(4,128)(2,1)S(1)} %pad_maximum_fusion), channel_id=1, replica_groups=mesh['kt'=8,'ks'=16] {'kt'}, dimensions={2}, use_global_device_ids=true | all-gather | bytes 442368 | tf_op jit(solution)/shard_map/all_gather | solution.py:36
  130.7 0.4 split.8
  131.1 0.3 copy.113
  131.4 0.1 copy.112
  131.5 0.3 copy.111
  131.8 0.1 copy.86
  131.9 0.2 copy.90
  132.1 0.4 reshape_reshape.3
  132.5 0.7 convert_bitcast_fusion
  133.2 12.2 %copy.103 = bf16[4,16,32,512,1]{2,1,0,4,3:T(8,128)(2,1)} copy(bf16[4,16,32,512,1]{3,2,1,0,4:T(8,128)(2,1)S(1)} %convert_bitcast_fusion) | data formatting | bytes 4194304 | tf_op jit(solution)/shard_map/convert_element_type | solution.py:73
  145.3 0.0 all-to-all-done.1
  145.3 5.6 %copy.96 = bf16[8,128,4,512]{3,2,1,0:T(4,128)(2,1)} copy(bf16[8,128,4,512]{3,2,0,1:T(4,128)(2,1)} %all-to-all-done.1) | data formatting | bytes 8388608 | tf_op jit(solution)/shard_map/all_to_all | solution.py:68
  150.9 6.9 %reshape.88 = bf16[2,4,512,512,1]{3,2,1,0,4:T(8,128)(2,1)} reshape(bf16[8,128,4,512]{3,2,1,0:T(4,128)(2,1)} %copy.96) | data formatting | bytes 8388608 | tf_op jit(solution)/shard_map/reshape | solution.py:69
  157.8 8.9 %fusion.3 = bf16[2,4,32,32,512]{4,3,2,1,0:T(8,128)(2,1)} fusion(f32[4,32,512]{2,1,0:T(8,128)S(1)} %convert_element_type.54, f32[2,32,512]{2,1,0:T(8,128)S(1)} %convert_bitcast_fusion.1, bf16[2,4,512,512,1]{3,2,1,0,4:T(8,128)(2,1)} %reshape.88), kind=kOutput, calls=%fused_computation.6 | convolution fusion | flops 4307550208 | bytes 12976128 | tf_op jit(solution)/shard_map/tsvwp,tspq->tsvwq/dot_general | solution.py:78
  166.8 44.3 %copy.98 = bf16[2,4,32,32,512]{3,2,1,0,4:T(8,128)(2,1)} copy(bf16[2,4,32,32,512]{4,3,2,1,0:T(8,128)(2,1)} %fusion.3) | data formatting | bytes 16777216 | tf_op jit(solution)/shard_map/convert_element_type | solution.py:80
  211.1 28.3 %fusion.4 = bf16[2,32,16,512]{1,2,0,3:T(8,128)(2,1)} fusion(bf16[4,16,32,512,1]{2,1,0,4,3:T(8,128)(2,1)} %copy.103, bf16[2,4,32,32,512]{3,2,1,0,4:T(8,128)(2,1)} %copy.98), kind=kOutput, calls=%fused_computation.7 | convolution fusion | flops 134742016 | bytes 11534336 | tf_op jit(solution)/shard_map/tsvwq,snwq->tvnq/dot_general | solution.py:81
  239.4 3.7 %fusion.11 = bf16[2,16,32,64]{3,2,1,0:T(8,128)(2,1)S(1)} fusion(bf16[2,64,512,1]{2,1,3,0:T(8,128)(2,1)S(1)} %bitcast.58, bf16[2,32,16,512]{1,2,0,3:T(8,128)(2,1)} %fusion.4), kind=kOutput, calls=%fused_computation.13 | convolution fusion | flops 67174400 | bytes 1310720 | tf_op jit(solution)/shard_map/tvnq,tcq->tnvc/dot_general | solution.py:84
  243.1 0.3 convert_element_type.61
  243.4 0.1 copy.121
  243.5 14.2 %all_to_all.15 = bf16[16,2,1,2048]{3,1,2,0:T(2,128)(2,1)S(1)} all-to-all(bf16[16,2,1,2048]{3,1,2,0:T(2,128)(2,1)S(1)} %bitcast.60), channel_id=1, replica_groups=mesh['kt'=8,'ks'=16] {'ks'}, dimensions={0} | all-to-all | bytes 262144 | tf_op jit(solution)/shard_map/all_to_all | solution.py:46
  257.7 0.1 convert_reduce_fusion
  257.8 0.6 reduce_sum.12
  258.5 0.0 copy-done.1
  (8 shorter events, 0.1 us)
Async XLA Ops:
  0.0 11.2 %copy-start = (bf16[512,4,512]{2,1,0:T(4,128)(2,1)S(1)}, bf16[512,4,512]{2,1,0:T(4,128)(2,1)}, u32[]{:S(2)}) copy-start(bf16[512,4,512]{2,1,0:T(4,128)(2,1)} %param.12) | copy-start | bytes 6291460
  1.8 26.7 %all-to-all-start = ((bf16[8,4,2,2048]{3,2,1,0:T(2,128)(2,1)}), bf16[8,4,2,2048]{3,2,1,0:T(2,128)(2,1)S(1)}, u32[]{:S(2)}, u32[]{:S(2)}) async-start(bf16[8,4,2,2048]{3,2,1,0:T(2,128)(2,1)} %stack.2), calls=%async_computation | async-start | bytes 524288 | tf_op jit(solution)/shard_map/all_to_all | solution.py:12
  28.5 10.9 %copy-start.5 = (bf16[2,64,32]{1,2,0:T(8,128)(2,1)S(1)}, bf16[2,64,32]{1,2,0:T(8,128)(2,1)}, u32[]{:S(2)}) copy-start(bf16[2,64,32]{1,2,0:T(8,128)(2,1)} %param.8) | copy-start | bytes 24580
  28.5 11.0 %copy-start.4 = (bf16[2,32,32]{2,1,0:T(8,128)(2,1)S(1)}, bf16[2,32,32]{2,1,0:T(8,128)(2,1)}, u32[]{:S(2)}) copy-start(bf16[2,32,32]{2,1,0:T(8,128)(2,1)} %param.7) | copy-start | bytes 12292
  28.5 71.2 %copy-start.3 = (bf16[4,32,64]{2,1,0:T(8,128)(2,1)S(1)}, bf16[4,32,64]{2,1,0:T(8,128)(2,1)}, u32[]{:S(2)}) copy-start(bf16[4,32,64]{2,1,0:T(8,128)(2,1)} %param.9) | copy-start | bytes 49156
  28.5 71.4 %copy-start.2 = (bf16[4,64,64]{2,1,0:T(8,128)(2,1)S(1)}, bf16[4,64,64]{2,1,0:T(8,128)(2,1)}, u32[]{:S(2)}) copy-start(bf16[4,64,64]{2,1,0:T(8,128)(2,1)} %param.10) | copy-start | bytes 98308
  28.5 116.8 %all-to-all-start.1 = ((bf16[8,128,4,512]{3,2,0,1:T(4,128)(2,1)}), bf16[8,128,4,512]{3,2,0,1:T(4,128)(2,1)}, u32[]{:S(2)}, u32[]{:S(2)}) async-start(bf16[8,128,4,512]{3,2,0,1:T(4,128)(2,1)} %copy.95), calls=%async_computation.1 | async-start | bytes 8388608 | tf_op jit(solution)/shard_map/all_to_all | solution.py:68
  211.1 47.4 %copy-start.1 = (bf16[512,4,512]{2,1,0:T(4,128)(2,1)S(1)}, bf16[512,4,512]{2,1,0:T(4,128)(2,1)}, u32[]{:S(2)}) copy-start(bf16[512,4,512]{2,1,0:T(4,128)(2,1)} %param.12) | copy-start | bytes 6291460
